TPU v7x, 32 devices: a whole 2x2x4 slice. The times are simulated.
32 devices in a mesh: row: 4 (over z), col: 2 (over x), depth: 4 (over y, core).
Axes of the slice: x: 2, y: 2, z: 4, core: 2. Of those that a mesh axis runs over, the one named last changes fastest.
Arguments:
- amplitudes: bfloat16 [3200, 7200], P('row', ('col', 'depth')), may hold values from -6 to 6
- integrals: bfloat16 [7200, 4096], P('row', ('col', 'depth')), may hold values from -0.0625 to 0.0625
- cycle_integrals: bfloat16 [256, 256], P('row'), as said below
- occ_irrep: int32 [100], replicated, may hold values from 0 to 7
- vir_irrep: int32 [900], replicated, may hold values from 0 to 7
Outputs:
- ladder: bfloat16 [3200, 4096], P('row', ('col', 'depth'))
- cycle: bfloat16 [256, 57600], P('row', ('col', 'depth'))
Inputs may be any that keep to these rules, and one draw needn't show every extreme that they name: cycle_integrals equals its transpose.
All inputs are finite; a program needn't handle non-finite values.
Results may differ from a plain program's by a relative error of at most 0.001.
Values may be sent and summed in bfloat16 or wider, within the bound.
A program may use at most 128 MiB of HBM per device.

v0:
```python
import jax
import jax.numpy as jnp
from jax import lax
from jax.sharding import PartitionSpec as P

NO = 100
NV = 900
JW = 64
CW = 8


def label_bits(labels):
    return jnp.stack([labels % 2, labels // 2 % 2, labels // 4 % 2])


def lookup(lookup_table, indices):
    matches = indices[:, None] == jnp.arange(lookup_table.shape[0], dtype=jnp.int32)[None, :]
    return jnp.sum(jnp.where(matches, lookup_table[None, :], 0), axis=1)


def shards(amplitudes, integrals, cycle_integrals, occ_irrep, vir_irrep):
    rows_here = amplitudes.shape[0]
    occ_block = rows_here // NO
    local_cols = amplitudes.shape[1]
    regroup_in = amplitudes.reshape(occ_block, NO, local_cols)[:, :JW, :]
    spread = lax.all_to_all(regroup_in, ("col", "depth"), split_axis=1, concat_axis=2, tiled=True)
    occ_here = spread.shape[1]
    ordered = (
        spread.reshape(occ_block, occ_here, CW, NV)
        .transpose(0, 2, 1, 3)
        .reshape(occ_block * CW, occ_here * NV)
    )
    columns = occ_here * NV
    integ_all = lax.all_gather(integrals, "row", axis=0, tiled=True)
    ladder_sum = jnp.dot(
        lax.all_gather(amplitudes, ("col", "depth"), axis=1, tiled=True),
        integ_all,
        preferred_element_type=jnp.float32,
    )
    ladder = ladder_sum.astype(jnp.bfloat16)
    cycle_rows_here = cycle_integrals.shape[0]
    cycle_sum = lax.psum_scatter(
        lax.dot_general(
            cycle_integrals, ordered, (((0,), (0,)), ((), ())), preferred_element_type=jnp.float32
        ),
        "row",
        scatter_dimension=0,
        tiled=True,
    )
    occ_bits = label_bits(occ_irrep)
    vir_bits = label_bits(vir_irrep)
    row_ids = lax.axis_index("row") * cycle_rows_here + jnp.arange(cycle_rows_here, dtype=jnp.int32)
    column_ids = lax.axis_index(("col", "depth")) * columns + jnp.arange(columns, dtype=jnp.int32)
    occ_first = row_ids // CW
    virt_first = row_ids % CW
    occ_second = column_ids // NV
    virt_second = column_ids % NV
    odd_count = jnp.zeros((cycle_rows_here, columns), jnp.int32)
    for digit in range(3):
        row_bits = lookup(occ_bits[digit], occ_first) + lookup(vir_bits[digit], virt_first)
        column_bits = lookup(occ_bits[digit], occ_second) + lookup(vir_bits[digit], virt_second)
        odd_count = odd_count + (row_bits[:, None] + column_bits[None, :]) % 2
    cycle = jnp.where(odd_count == 0, cycle_sum, jnp.float32(0.0)).astype(jnp.bfloat16)
    return (ladder, cycle)


def solution(mesh):
    in_specs = (P("row", ("col", "depth")), P("row", ("col", "depth")), P("row", None), P(), P())
    out_specs = (P("row", ("col", "depth")), P("row", ("col", "depth")))
    return jax.shard_map(shards, mesh=mesh, in_specs=in_specs, out_specs=out_specs, check_vma=False)
```

profile of v0, /device:TPU:0, one launch (start us, length us, event | category | flops | bytes accessed | tf_op | source)
XLA Modules:
  0.0 310.4 jit_solution(11669424504243657550)
XLA Ops:
  8.0 0.0 copy-start
  8.0 0.0 reduce-scatter.2.cloned.1.call-start
  8.1 3.8 %reshape.104 = bf16[8,100,900]{1,0,2:T(8,128)(2,1)S(1)} reshape(bf16[800,900]{0,1:T(8,128)(2,1)} %param.5) | data formatting | bytes 2880000 | tf_op jit(solution)/shard_map/reshape | solution.py:25
  11.8 2.8 copy.15
  14.7 19.6 %all_to_all.4 = bf16[8,64,900]{2,0,1:T(8,128)(2,1)S(1)} all-to-all(bf16[8,64,900]{2,0,1:T(8,128)(2,1)S(1)} %copy.15), channel_id=1, replica_groups=mesh['row'=4,'col'=2,'depth'=4] {'col','depth'}, dimensions={1} | all-to-all | bytes 1843200 | tf_op jit(solution)/shard_map/all_to_all | solution.py:26
  34.3 0.6 copy.16
  34.9 1.3 reshape.100
  36.2 0.0 copy-done
  36.2 4.2 %fusion.18 = f32[256,7200]{1,0:T(8,128)} fusion(bf16[64,256]{1,0:T(8,128)(2,1)S(1)} %copy-done, bf16[64,7200]{1,0:T(8,128)(2,1)S(1)} %reshape.100), kind=kOutput, calls=%fused_computation.91 | convolution fusion | flops 235929600 | bytes 8327168 | tf_op jit(solution)/shard_map/dot_general | solution.py:43
  40.4 0.0 reduce-scatter.2.cloned.1.call-update
  40.4 0.0 copy-start.2
  40.4 0.0 copy-start.1
  40.5 0.0 all-gather.6.cloned.1.call-start
  40.5 0.5 all-gather.6.cloned.1.call-update
  41.0 0.2 all-gather.4.cloned.1.call-start
  41.3 0.4 all-gather.4.cloned.1.call-update
  41.7 0.0 copy-done.2
  41.7 0.0 copy-done.1
  41.7 1.1 select_reduce_fusion.5
  42.9 9.3 %select_reduce_fusion.2 = (s32[7200]{0:T(1024)S(1)}, s32[7200]{0:T(1024)S(1)}, s32[7200]{0:T(1024)S(1)}) fusion(s32[900]{0:T(1024)S(1)} %get-tuple-element.16, s32[7200]{0:T(1024)S(1)} %get-tuple-element.20, s32[900]{0:T(1024)S(1)} %get-tuple-element.15, s32[900]{0:T(1024)S(1)} %get-tuple-element.14), kind=kLoop, calls=%fused_computation.2 | loop fusion | flops 45338400 | bytes 126000 | tf_op jit(solution)/shard_map/reduce_sum | solution.py:18
  52.2 0.2 select_reduce_fusion.11
  52.4 0.3 select_reduce_fusion.8
  52.8 157.8 %reduce-scatter.2.cloned.1.call-done = f32[64,7200]{1,0:T(8,128)} async-done(((f32[256,7200]{1,0:T(8,128)}), f32[64,7200]{1,0:T(8,128)}) %reduce-scatter.2.cloned.1.call-update) | async-done | bytes 1843216 | tf_op jit(solution)/shard_map/reduce_scatter | solution.py:42
  210.5 4.6 %select_convert_fusion = bf16[64,7200]{1,0:T(8,128)(2,1)} fusion(f32[64,7200]{1,0:T(8,128)} %reduce-scatter.2.cloned.1.call-done, s32[7200]{0:T(1024)S(1)} %add.222, s32[64]{0:T(128)S(1)} %add.220, s32[7200]{0:T(1024)S(1)} %add.213, s32[64]{0:T(128)S(1)} %add.211, s32[7200]{0:T(1024)S(1)} %add.205, s32[64]{0:T(128)S(1)} %add.199), kind=kLoop, calls=%fused_computation.29 | loop fusion | flops 18432000 | bytes 2851968 | tf_op jit(solution)/shard_map/convert_element_type | solution.py:63
  215.1 0.0 all-gather.6.cloned.1.call-done
  215.1 12.2 %reshape.103 = bf16[7200,800]{1,0:T(8,128)(2,1)} reshape(bf16[8,900,800]{2,1,0:T(8,128)(2,1)} %all-gather.6.cloned.1.call-done) | data formatting | bytes 23040000
  227.3 61.8 %all-gather.4.cloned.1.call-done = bf16[7200,512]{1,0:T(8,128)(2,1)} async-done(((bf16[1800,512]{1,0:T(8,128)(2,1)}), bf16[7200,512]{1,0:T(8,128)(2,1)}) %all-gather.4.cloned.1.call-update) | async-done | bytes 7372816 | tf_op jit(solution)/shard_map/all_gather | solution.py:34
  289.1 13.9 %convolution_convert_fusion = bf16[800,512]{1,0:T(8,128)(2,1)} fusion(bf16[7200,800]{1,0:T(8,128)(2,1)} %reshape.103, bf16[7200,512]{1,0:T(8,128)(2,1)} %all-gather.4.cloned.1.call-done), kind=kOutput, calls=%fused_computation.30 | convolution fusion | flops 5898649600 | bytes 19712000 | tf_op jit(solution)/shard_map/dot_general | solution.py:35
  (10 shorter events, 0.1 us)
Async XLA Ops:
  8.0 28.2 %copy-start = (bf16[64,256]{1,0:T(8,128)(2,1)S(1)}, bf16[64,256]{1,0:T(8,128)(2,1)}, u32[]{:S(2)}) copy-start(bf16[64,256]{1,0:T(8,128)(2,1)} %param.7) | copy-start | bytes 98308
  8.0 202.5 %reduce-scatter.2.cloned.1.call-start = ((), (), s32[]{:S(2)}) async-start(), calls=%async_computation.3 | async-start | bytes 9338880 | tf_op jit(solution)/shard_map/reduce_scatter | solution.py:42
  40.4 1.2 copy-start.2
  40.4 1.3 copy-start.1
  40.5 174.6 %all-gather.6.cloned.1.call-start = ((), (), s32[]{:S(2)}) async-start(), calls=%async_computation.4 | async-start | bytes 14579712 | tf_op jit(solution)/shard_map/all_gather | solution.py:36
  41.0 248.0 %all-gather.4.cloned.1.call-start = ((), (), s32[]{:S(2)}) async-start(), calls=%async_computation.2 | async-start | bytes 9216000 | tf_op jit(solution)/shard_map/all_gather | solution.py:34
Sparse Core Ops, SparseCore 0:
  40.5 169.9 reduce-scatter.1
Sparse Core Ops, SparseCore 1:
  42.8 73.7 all-gather.5
  118.0 171.0 all-gather.3
where the time goes:
time: 311 us; the launch traced here: 310 us
  waiting for transfers between devices  220 us (71%)
  local copies, waits for them, and re-layouts  20.7 us (7%)
  blocking collectives  19.6 us (6%)
  matrix products  18.1 us (6%)
  between operations  15.7 us (5%)
  other arithmetic  15.6 us (5%)
    reduce_scatter x1, waiting for transfers between devices, shards(): lax.psum_scatter(lax.dot_general(cycle_integrals, ordered, (((0,), (0,)),...  158 us
    all_gather x1, waiting for transfers between devices, shards(): integ_all = lax.all_gather(integrals, 'row', axis=0, tiled=True)  61.8 us
    all_to_all x1, blocking collectives, shards(): lax.all_to_all(regroup_in, ('col', 'depth'), split_axis=1, concat_axis=2,...  19.6 us
    dot_general x1, matrix products, shards(): jnp.dot(lax.all_gather(amplitudes, ('col', 'depth'), axis=1, tiled=True),...  13.9 us
    unnamed x7, local copies, waits for them, and re-layouts  12.2 us
    reduce_sum x4, other arithmetic, lookup(): return jnp.sum(jnp.where(matches, lookup_table[None, :], 0), axis=1)  10.9 us
  transfers between devices with their start and end apart: 3, of which 2 were waited for; matrix products, arithmetic and copies ran while one was open for 9% of the time, Pallas kernels for 0%

commit v1 on v0

v1 whole, which is shorter than its diff:
```python
import functools

import jax
import jax.numpy as jnp
from jax import lax
from jax.experimental import pallas as pl
from jax.experimental.pallas import tpu as pltpu
from jax.sharding import PartitionSpec as P

NO = 100
NV = 900
JW = 64
CW = 8
MESH = pl.DeviceIdType.MESH


def masks(rows_here, columns, occ_irrep, vir_irrep):
    occ_rows = rows_here // CW
    occ_cols = columns // NV
    occ_i = lax.dynamic_slice(occ_irrep, (lax.axis_index("row") * occ_rows,), (occ_rows,))
    occ_j = lax.dynamic_slice(occ_irrep, (lax.axis_index(("col", "depth")) * occ_cols,), (occ_cols,))
    row_label = (occ_i[:, None] ^ vir_irrep[None, :CW]).reshape(rows_here, 1)
    col_label = (occ_j[:, None] ^ vir_irrep[None, :]).reshape(1, columns)
    return row_label, col_label


def general(amplitudes, integrals, cycle_integrals, occ_irrep, vir_irrep):
    rows_here = amplitudes.shape[0]
    occ_block = rows_here // NO
    local_cols = amplitudes.shape[1]
    regroup_in = amplitudes.reshape(occ_block, NO, local_cols)[:, :JW, :]
    spread = lax.all_to_all(regroup_in, ("col", "depth"), split_axis=1, concat_axis=2, tiled=True)
    occ_here = spread.shape[1]
    columns = occ_here * NV
    ordered = (
        spread.reshape(occ_block, occ_here, CW, NV)
        .transpose(0, 2, 1, 3)
        .reshape(occ_block * CW, columns)
    )
    everyone = lax.all_gather(ordered, "row", axis=0, tiled=True)
    integ_all = lax.all_gather(integrals, "row", axis=0, tiled=True)
    ladder = jnp.dot(
        lax.all_gather(amplitudes, ("col", "depth"), axis=1, tiled=True),
        integ_all,
        preferred_element_type=jnp.float32,
    ).astype(jnp.bfloat16)
    cycle_sum = jnp.dot(cycle_integrals, everyone, preferred_element_type=jnp.float32)
    row_label, col_label = masks(cycle_integrals.shape[0], columns, occ_irrep, vir_irrep)
    cycle = jnp.where(row_label == col_label, cycle_sum, jnp.float32(0.0)).astype(jnp.bfloat16)
    return ladder, cycle


def kernel(nz, a_ref, b_ref, s_ref, ci_ref, rl_ref, cl_ref, lad_ref, cyc_ref,
           aall, ball, rall, acc, loc_sem, s_send, s_recv, a_send, a_recv, z_send, z_recv):
    z = lax.axis_index("row")
    x = lax.axis_index("col")
    dep = lax.axis_index("depth")
    y, core = dep // 2, lax.rem(dep, 2)
    nd = 4
    npl = 8
    p = x * nd + dep
    partner = {"depth": y * 2 + 1 - core}
    xn = {"col": 1 - x}
    yn = {"depth": (1 - y) * 2 + core}

    def remote(src, dst, ss, rs, dev):
        return pltpu.make_async_remote_copy(
            src_ref=src, dst_ref=dst, send_sem=ss, recv_sem=rs, device_id=dev, device_id_type=MESH
        )

    def peer(i):
        q = lax.rem(p + i, npl)
        return q, {"col": q // nd, "depth": lax.rem(q, nd)}

    barrier = pltpu.get_barrier_semaphore()
    for i in range(1, npl):
        pl.semaphore_signal(barrier, inc=1, device_id=peer(i)[1], device_id_type=MESH)

    @pl.when(z > 0)
    def _():
        pl.semaphore_signal(barrier, inc=1, device_id={"row": z - 1}, device_id_type=MESH)

    @pl.when(z < nz - 1)
    def _():
        pl.semaphore_signal(barrier, inc=1, device_id={"row": z + 1}, device_id_type=MESH)

    own_a = pltpu.make_async_copy(a_ref, aall.at[p], loc_sem.at[0])
    own_b = pltpu.make_async_copy(b_ref, ball.at[z], loc_sem.at[1])
    own_s = pltpu.make_async_copy(s_ref.at[p], rall.at[z, p], loc_sem.at[2])
    own_a.start()
    own_b.start()
    own_s.start()

    greeted = npl + 1 - (z == 0).astype(jnp.int32) - (z == nz - 1).astype(jnp.int32)
    pl.semaphore_wait(barrier, greeted)

    def z_dst(item, s):
        return rall.at[s] if item == 2 else ball.at[s, item]

    def z_copy(item, s, up, src=None):
        dst = z_dst(item, s)
        d = 1 if up else 0
        dev = {"row": z + 1} if up else {"row": z - 1}
        return remote(dst if src is None else src, dst, z_send.at[item, s, d], z_recv.at[item, s], dev)

    def z_out(item, s, up, start, src=None):
        edge = (z < nz - 1) if up else (z > 0)

        @pl.when(edge)
        def _():
            c = z_copy(item, s, up, src)
            if start:
                c.start()
            else:
                c.wait_send()

    def z_both(item, start, src=None):
        z_out(item, z, True, start, src)
        z_out(item, z, False, start, src)

    for i in range(1, npl):
        q, dev = peer(i)
        remote(s_ref.at[q], rall.at[z, p], s_send.at[i], s_recv.at[p], dev).start()
    z_both(0, True, b_ref.at[0])
    z_both(1, True, b_ref.at[1])

    def a_copy(q, h, way, src=None):
        dst = aall.at[q, h]
        k = {"p": 0, "x": 1, "y": 2}[way]
        dev = {"p": partner, "x": xn, "y": yn}[way]
        return remote(dst if src is None else src, dst, a_send.at[k, q, h], a_recv.at[q, h], dev)

    q_x = (1 - x) * nd + dep
    q_y = x * nd + (1 - y) * 2 + core
    q_d = (1 - x) * nd + (1 - y) * 2 + core
    sends = []

    def a_start(q, h, way, src=None):
        c = a_copy(q, h, way, src)
        c.start()
        sends.append(c)

    for h in range(2):
        for way in ("x", "y", "p"):
            a_start(p, h, way, a_ref.at[h])

    own_s.wait()
    for i in range(1, npl):
        q, dev = peer(i)
        remote(s_ref.at[p], rall.at[z, q], s_send.at[i], s_recv.at[q], dev).wait_recv()
    z_both(2, True)

    a_copy(q_x, 0, "x").wait_recv()
    a_start(q_x, 0, "y")
    a_start(q_x, 0, "p")
    a_copy(q_y, 0, "y").wait_recv()
    a_start(q_y, 0, "p")
    a_copy(q_y, 1, "y").wait_recv()
    a_start(q_y, 1, "x")
    a_start(q_y, 1, "p")
    a_copy(q_x, 1, "x").wait_recv()
    a_start(q_x, 1, "p")

    def arrive(item, dist):
        @pl.when(z - dist >= 0)
        def _():
            z_copy(item, z - dist, True).wait_recv()
            z_out(item, z - dist, True, True)

        @pl.when(z + dist < nz)
        def _():
            z_copy(item, z + dist, False).wait_recv()
            z_out(item, z + dist, False, True)

    arrive(0, 1)
    a_copy(q_d, 0, "y").wait_recv()
    a_start(q_d, 0, "p")
    a_copy(q_d, 1, "x").wait_recv()
    a_start(q_d, 1, "p")
    arrive(1, 1)
    for q in (p, q_x, q_y, q_d):
        other = q + 1 - 2 * core
        for h in range(2):
            a_copy(other, h, "p").wait_recv()
    own_a.wait()
    own_b.wait()
    per = npl // nz
    acc[...] = jnp.zeros_like(acc)

    def ladder_part(s, item):
        def body(n, carry):
            kb, h = n // 2, lax.rem(n, 2)
            acc[h, item] += jnp.dot(
                aall[s * per + kb, h], ball[s, item, kb], preferred_element_type=jnp.float32
            )
            return carry

        lax.fori_loop(0, 2 * per, body, 0)

    cols = cyc_ref.shape[1]
    width = 1024
    bounds = [(c, min(c + width, cols)) for c in range(0, cols, width)]

    ladder_part(z, 0)
    ladder_part(z, 1)

    def consume(item, dist):
        @pl.when(z - dist >= 0)
        def _():
            ladder_part(z - dist, item)

        @pl.when(z + dist < nz)
        def _():
            ladder_part(z + dist, item)

    for dist in range(1, nz):
        if dist > 1:
            arrive(0, dist)
            consume(0, dist)
            arrive(1, dist)
            consume(1, dist)
        else:
            consume(0, dist)
            consume(1, dist)
        arrive(2, dist)

    hr = lad_ref.shape[0] // 2
    hc = lad_ref.shape[1] // 2
    for h in range(2):
        for item in range(2):
            lad_ref[h * hr:(h + 1) * hr, item * hc:(item + 1) * hc] = acc[h, item].astype(lad_ref.dtype)
    rows = rall.shape[0] * rall.shape[1] * rall.shape[2]
    for lo, hi in bounds:
        r = rall[:, :, :, lo:hi].reshape(rows, hi - lo)
        total = jnp.dot(ci_ref[...], r, preferred_element_type=jnp.float32)
        keep = rl_ref[...] == cl_ref[:, lo:hi]
        cyc_ref[:, lo:hi] = jnp.where(keep, total, 0.0).astype(cyc_ref.dtype)

    for i in range(1, npl):
        q, dev = peer(i)
        remote(s_ref.at[q], rall.at[z, p], s_send.at[i], s_recv.at[p], dev).wait_send()
    for c in sends:
        c.wait_send()
    z_both(0, False, b_ref.at[0])
    z_both(1, False, b_ref.at[1])
    z_both(2, False)
    for dist in range(1, nz):
        for item in range(3):
            @pl.when(z - dist >= 0)
            def _():
                z_out(item, z - dist, True, False)

            @pl.when(z + dist < nz)
            def _():
                z_out(item, z + dist, False, False)


def shards(nz, npl, amplitudes, integrals, cycle_integrals, occ_irrep, vir_irrep):
    rows, kb = amplitudes.shape
    occ = rows // NO
    n = integrals.shape[1]
    per = npl // nz
    occ_here = JW // npl
    columns = occ_here * NV
    crow = cycle_integrals.shape[0]
    a = amplitudes.reshape(2, rows // 2, kb)
    b = integrals.reshape(per, kb, 2, n // 2).transpose(2, 0, 1, 3)
    s = (
        amplitudes.reshape(occ, NO, kb)[:, :JW]
        .reshape(occ, npl, occ_here, kb)
        .transpose(1, 0, 2, 3)
        .reshape(npl, occ, columns)
    )
    ci = cycle_integrals.reshape(crow, nz, occ, CW).transpose(0, 1, 3, 2).reshape(crow, -1)
    row_label, col_label = masks(crow, columns, occ_irrep, vir_irrep)
    bf = jnp.bfloat16
    dma = pltpu.SemaphoreType.DMA
    return pl.pallas_call(
        functools.partial(kernel, nz),
        out_shape=(
            jax.ShapeDtypeStruct((rows, n), bf),
            jax.ShapeDtypeStruct((crow, columns), bf),
        ),
        in_specs=[pl.BlockSpec(memory_space=pltpu.VMEM)] * 6,
        out_specs=(pl.BlockSpec(memory_space=pltpu.VMEM),) * 2,
        scratch_shapes=[
            pltpu.VMEM((npl, 2, rows // 2, kb), bf),
            pltpu.VMEM((nz, 2, per, kb, n // 2), bf),
            pltpu.VMEM((nz, npl, occ, columns), bf),
            pltpu.VMEM((2, 2, rows // 2, n // 2), jnp.float32),
            dma((3,)),
            dma((npl,)),
            dma((npl,)),
            dma((3, npl, 2)),
            dma((npl, 2)),
            dma((3, nz, 2)),
            dma((3, nz)),
        ],
        compiler_params=pltpu.CompilerParams(
            collective_id=0, has_side_effects=True, vmem_limit_bytes=60 * 1024 * 1024
        ),
    )(a, b, s, ci, row_label, col_label)


def solution(mesh):
    nz, nx, nd = mesh.shape["row"], mesh.shape["col"], mesh.shape["depth"]
    npl = nx * nd
    if nx == 2 and nd == 4 and npl == CW and npl % nz == 0:
        body = functools.partial(shards, nz, npl)
    else:
        body = general
    in_specs = (P("row", ("col", "depth")), P("row", ("col", "depth")), P("row", None), P(), P())
    out_specs = (P("row", ("col", "depth")), P("row", ("col", "depth")))
    return jax.shard_map(body, mesh=mesh, in_specs=in_specs, out_specs=out_specs, check_vma=False)
```

time: 311 us -> 209 us (0.67)
  waiting for transfers between devices: 220 us -> 0 us
  Pallas kernels: 0 us -> 191 us
  blocking collectives: 19.6 us -> 0 us
  matrix products: 18.1 us -> 0 us
  other arithmetic: 15.6 us -> 0.14 us
  between operations: 15.7 us -> 0.74 us
  local copies, waits for them, and re-layouts: 20.7 us -> 17 us
    pallas_call x0 -> x1, Pallas kernels: none -> 191 us  [shards(): pl.pallas_call(functools.partial(kernel, nz), out_shape=(jax.ShapeDtypeSt...]
    reduce_scatter x1 -> x0, waiting for transfers between devices: 158 us -> none  [shards(): lax.psum_scatter(lax.dot_general(cycle_integrals, ordered, (((0,), (0,)),...]
    all_gather x2 -> x0, waiting for transfers between devices: 61.8 us -> none  [the longest x1 61.8 us: shards(): integ_all = lax.all_gather(integrals, 'row', axis=0, tiled=True)]
    all_to_all x1 -> x0, blocking collectives: 19.6 us -> none  [shards(): lax.all_to_all(regroup_in, ('col', 'depth'), split_axis=1, concat_axis=2,...]
    dot_general x2 -> x0, matrix products: 18.1 us -> none  [the longest x1 13.9 us: shards(): jnp.dot(lax.all_gather(amplitudes, ('col', 'depth'), axis=1, tiled=True),...]
    reduce_sum x4 -> x0, other arithmetic: 10.9 us -> none  [lookup(): return jnp.sum(jnp.where(matches, lookup_table[None, :], 0), axis=1)]
    unnamed x7 -> x14, local copies, waits for them, and re-layouts: 12.2 us -> 5.99 us
    convert_element_type x1 -> x0, other arithmetic: 4.55 us -> none  [shards(): jnp.where(odd_count == 0, cycle_sum, jnp.float32(0.0)).astype(jnp.bfloat16)]
  transfers between devices with their start and end apart: 3 -> 0, of which waited for: 2 -> 0; matrix products, arithmetic and copies ran while one was open for 9% -> 0% of each run, Pallas kernels for 0% -> 0%
where the time goes in v1:
time: 209 us
  Pallas kernels  191 us (91%)
  local copies, waits for them, and re-layouts  17 us (8%)
    pallas_call x1, Pallas kernels, shards(): pl.pallas_call(functools.partial(kernel, nz), out_shape=(jax.ShapeDtypeSt...  191 us
    unnamed x14, local copies, waits for them, and re-layouts  5.99 us
    reshape x2, local copies, waits for them, and re-layouts, shards(): b = integrals.reshape(per, kb, 2, n // 2).transpose(2, 0, 1, 3)  5.93 us

profile of v1, /device:TPU:0, one launch (start us, length us, event | category | flops | bytes accessed | tf_op | source)
XLA Modules:
  0.0 208.8 jit_solution(9216981874099415251)
XLA Ops:
  0.6 2.8 %copy.10 = bf16[800,900]{1,0:T(8,128)(2,1)S(1)} copy(bf16[800,900]{0,1:T(8,128)(2,1)} %param.5) | data formatting | bytes 2880000 | tf_op args[0]
  3.4 0.0 copy-start
  3.4 4.4 %reshape.76 = bf16[2,900,2,256]{3,2,1,0:T(2,128)(2,1)S(1)} reshape(bf16[1800,512]{1,0:T(8,128)(2,1)} %param.6) | data formatting | bytes 3686400 | tf_op jit(solution)/shard_map/reshape | solution.py:267
  7.8 1.5 copy.20
  9.3 0.0 copy-done
  9.3 0.4 reshape.77
  9.8 0.1 slice_bitcast_fusion
  9.9 0.0 copy-start.2
  9.9 0.0 copy-start.4
  9.9 0.0 slice-start
  9.9 0.0 copy-start.3
  9.9 1.3 reshape.82
  11.2 1.0 copy.18.s_ref
  12.2 0.0 copy-done.2
  12.2 0.1 copy.14
  12.4 0.7 copy.16.ci_ref
  13.1 0.0 copy-done.4
  13.1 0.1 fusion
  13.2 0.0 slice-done
  13.2 0.1 broadcast_xor_fusion.1
  13.2 0.7 xor.54.rl_ref
  13.9 0.0 copy-done.3
  13.9 0.1 broadcast_xor_fusion
  14.0 0.7 xor.53.cl_ref
  14.7 191.0 %shard_map.68 = (bf16[800,512]{1,0:T(8,128)(2,1)}, bf16[64,7200]{1,0:T(8,128)(2,1)}) custom-call(bf16[2,400,900]{2,1,0:T(8,128)(2,1)} %bitcast.16, bf16[2,2,900,256]{3,2,1,0:T(8,128)(2,1)} %bitcast.17, bf16[8,8,7200]{2,1,0:T(8,128)(2,1)} %copy.18.s_ref, bf16[64,256]{1,0:T(8,128)(2,1)} %copy.16.ci_ref, s32[64,1]{1,0:T(8,128)} %xor.54.rl_ref, ...), custom_call_target="tpu_custom_call" | custom-call | tf_op jit(solution)/shard_map/pallas_call | solution.py:278
  205.7 0.0 copy-start.1
  205.7 2.2 %copy.23 = bf16[800,512]{1,0:T(8,128)(2,1)} copy(bf16[800,512]{1,0:T(8,128)(2,1)} %get-tuple-element.6) | data formatting | bytes 1638400
  207.9 0.0 copy-done.1
  207.9 0.9 copy.24
  (1 shorter events, 0.0 us)
Async XLA Ops:
  3.4 6.0 %copy-start = (bf16[800,900]{1,0:T(8,128)(2,1)}, bf16[800,900]{1,0:T(8,128)(2,1)S(1)}, u32[]{:S(2)}) copy-start(bf16[800,900]{1,0:T(8,128)(2,1)S(1)} %copy.10) | copy-start | bytes 4320004
  9.9 2.4 %copy-start.2 = (bf16[64,256]{1,0:T(8,128)(2,1)S(1)}, bf16[64,256]{1,0:T(8,128)(2,1)}, u32[]{:S(2)}) copy-start(bf16[64,256]{1,0:T(8,128)(2,1)} %param.7) | copy-start | bytes 98308
  9.9 3.2 %copy-start.4 = (s32[100]{0:T(128)S(1)}, s32[100]{0:T(128)}, u32[]{:S(2)}) copy-start(s32[100]{0:T(128)} %param.8) | copy-start | bytes 1204
  9.9 3.3 %slice-start = ((s32[900]{0:T(1024)}), s32[8]{0:T(128)S(1)}, s32[]{:S(2)}) async-start(s32[900]{0:T(1024)} %param.9), calls=%async_computation | async-start | bytes 1024 | tf_op jit(solution)/shard_map/slice | solution.py:22
  9.9 4.0 %copy-start.3 = (s32[900]{0:T(1024)S(1)}, s32[900]{0:T(1024)}, u32[]{:S(2)}) copy-start(s32[900]{0:T(1024)} %param.9) | copy-start | bytes 10804
  205.7 2.2 %copy-start.1 = (bf16[64,7200]{1,0:T(8,128)(2,1)S(1)}, bf16[64,7200]{1,0:T(8,128)(2,1)}, u32[]{:S(2)}) copy-start(bf16[64,7200]{1,0:T(8,128)(2,1)} %get-tuple-element.7) | copy-start | bytes 2764804

commit v2 on v1

v2 whole, which is shorter than its diff:
```python
import functools

import jax
import jax.numpy as jnp
from jax import lax
from jax.experimental import pallas as pl
from jax.experimental.pallas import tpu as pltpu
from jax.sharding import PartitionSpec as P

NO = 100
NV = 900
JW = 64
CW = 8
MESH = pl.DeviceIdType.MESH


def masks(rows_here, columns, occ_irrep, vir_irrep):
    occ_rows = rows_here // CW
    occ_cols = columns // NV
    occ_i = lax.dynamic_slice(occ_irrep, (lax.axis_index("row") * occ_rows,), (occ_rows,))
    occ_j = lax.dynamic_slice(occ_irrep, (lax.axis_index(("col", "depth")) * occ_cols,), (occ_cols,))
    row_label = (occ_i[:, None] ^ vir_irrep[None, :CW]).reshape(rows_here, 1)
    col_label = (occ_j[:, None] ^ vir_irrep[None, :]).reshape(1, columns)
    return row_label, col_label


def general(amplitudes, integrals, cycle_integrals, occ_irrep, vir_irrep):
    rows_here = amplitudes.shape[0]
    occ_block = rows_here // NO
    local_cols = amplitudes.shape[1]
    regroup_in = amplitudes.reshape(occ_block, NO, local_cols)[:, :JW, :]
    spread = lax.all_to_all(regroup_in, ("col", "depth"), split_axis=1, concat_axis=2, tiled=True)
    occ_here = spread.shape[1]
    columns = occ_here * NV
    ordered = (
        spread.reshape(occ_block, occ_here, CW, NV)
        .transpose(0, 2, 1, 3)
        .reshape(occ_block * CW, columns)
    )
    everyone = lax.all_gather(ordered, "row", axis=0, tiled=True)
    integ_all = lax.all_gather(integrals, "row", axis=0, tiled=True)
    ladder = jnp.dot(
        lax.all_gather(amplitudes, ("col", "depth"), axis=1, tiled=True),
        integ_all,
        preferred_element_type=jnp.float32,
    ).astype(jnp.bfloat16)
    cycle_sum = jnp.dot(cycle_integrals, everyone, preferred_element_type=jnp.float32)
    row_label, col_label = masks(cycle_integrals.shape[0], columns, occ_irrep, vir_irrep)
    cycle = jnp.where(row_label == col_label, cycle_sum, jnp.float32(0.0)).astype(jnp.bfloat16)
    return ladder, cycle


def kernel(a_ref, b_ref, s_ref, ci_ref, rl_ref, cl_ref, lad_ref, cyc_ref,
           aall, oall, ball, rall, acc, pacc, pin, loc_sem, s_send, s_recv,
           a_send, a_recv, o_send, o_recv, z_send, z_recv, n_send, p_send, p_recv):
    z = lax.axis_index("row")
    x = lax.axis_index("col")
    dep = lax.axis_index("depth")
    y, core = dep // 2, lax.rem(dep, 2)
    nd = 4
    npl = 8
    nz = rall.shape[0]
    per = npl // nz
    p = x * nd + dep
    partner = {"depth": y * 2 + 1 - core}
    xn = {"col": 1 - x}
    yn = {"depth": (1 - y) * 2 + core}
    inward = jnp.where(z < nz // 2, 1, -1)
    outer = (z == 0) | (z == nz - 1)
    inner = jnp.logical_not(outer)
    to_in = {"row": z + inward}
    to_out = {"row": z - inward}

    def remote(src, dst, ss, rs, dev):
        return pltpu.make_async_remote_copy(
            src_ref=src, dst_ref=dst, send_sem=ss, recv_sem=rs, device_id=dev, device_id_type=MESH
        )

    def peer(i):
        q = lax.rem(p + i, npl)
        return q, {"col": q // nd, "depth": lax.rem(q, nd)}

    barrier = pltpu.get_barrier_semaphore()
    for i in range(1, npl):
        pl.semaphore_signal(barrier, inc=1, device_id=peer(i)[1], device_id_type=MESH)
    pl.semaphore_signal(barrier, inc=1, device_id=to_in, device_id_type=MESH)

    @pl.when(inner)
    def _():
        pl.semaphore_signal(barrier, inc=1, device_id=to_out, device_id_type=MESH)

    own_a = pltpu.make_async_copy(a_ref, aall.at[p], loc_sem.at[0])
    own_b = pltpu.make_async_copy(b_ref, ball.at[z], loc_sem.at[1])
    own_s = pltpu.make_async_copy(s_ref.at[p], rall.at[z, p], loc_sem.at[2])
    own_a.start()
    own_b.start()
    own_s.start()
    pl.semaphore_wait(barrier, npl + inner.astype(jnp.int32))

    common, middle, ends = [], [], []

    def begin(kept, make, *args, **kw):
        make(*args, **kw).start()
        kept.append(functools.partial(make, *args, **kw))

    def z_copy(item, k, outwards=False, src=None):
        s = z + k * inward
        dst = rall.at[s] if item == 2 else ball.at[s, item]
        d = 1 if outwards else 0
        return remote(dst if src is None else src(), dst, z_send.at[item, s, d],
                      z_recv.at[item, s], to_out if outwards else to_in)

    def arrived(item, k):
        z_copy(item, k).wait_recv()

    def o_in(h):
        return remote(a_ref.at[h], oall.at[p, h], n_send.at[h], o_recv.at[p, h], to_in)

    def s_out(i):
        q, dev = peer(i)
        return remote(s_ref.at[q], rall.at[z, p], s_send.at[i], s_recv.at[p], dev)

    for i in range(1, npl):
        begin(common, s_out, i)

    @pl.when(outer)
    def _():
        for h in range(2):
            begin(ends, o_in, h)

    begin(common, z_copy, 1, 0, src=lambda: b_ref.at[1])

    @pl.when(inner)
    def _():
        begin(middle, z_copy, 1, 0, True, src=lambda: b_ref.at[1])

    q_x = (1 - x) * nd + dep
    q_y = x * nd + (1 - y) * 2 + core
    q_d = (1 - x) * nd + (1 - y) * 2 + core

    def plane(buf, send, recv, kept):
        def copy(q, h, way, src=None):
            n = {"p": 0, "x": 1, "y": 2}[way]
            dev = {"p": partner, "x": xn, "y": yn}[way]
            dst = buf.at[q, h]
            return remote(dst if src is None else src(), dst, send.at[n, q, h], recv.at[q, h], dev)

        def first(src):
            for h in range(2):
                for way in ("x", "y", "p"):
                    begin(kept, copy, p, h, way, functools.partial(src, h))

        def second():
            copy(q_x, 0, "x").wait_recv()
            begin(kept, copy, q_x, 0, "y")
            begin(kept, copy, q_x, 0, "p")
            copy(q_y, 0, "y").wait_recv()
            begin(kept, copy, q_y, 0, "p")
            copy(q_y, 1, "y").wait_recv()
            begin(kept, copy, q_y, 1, "x")
            begin(kept, copy, q_y, 1, "p")
            copy(q_x, 1, "x").wait_recv()
            begin(kept, copy, q_x, 1, "p")

        def third():
            copy(q_d, 0, "y").wait_recv()
            begin(kept, copy, q_d, 0, "p")
            copy(q_d, 1, "x").wait_recv()
            begin(kept, copy, q_d, 1, "p")

        def last():
            for q in (p, q_x, q_y, q_d):
                other = q + 1 - 2 * core
                for h in range(2):
                    copy(other, h, "p").wait_recv()

        return first, second, third, last

    a_first, a_second, a_third, a_last = plane(aall, a_send, a_recv, common)
    o_first, o_second, o_third, o_last = plane(oall, o_send, o_recv, middle)

    a_first(lambda h: a_ref.at[h])

    own_s.wait()
    for i in range(1, npl):
        q, dev = peer(i)
        remote(s_ref.at[p], rall.at[z, q], s_send.at[i], s_recv.at[q], dev).wait_recv()
    begin(common, z_copy, 2, 0)

    @pl.when(inner)
    def _():
        begin(middle, z_copy, 2, 0, True)

    begin(common, z_copy, 0, 0, src=lambda: b_ref.at[0])

    a_second()
    acc[...] = jnp.zeros_like(acc)
    pacc[...] = jnp.zeros_like(pacc)

    def ladder_part(k, item):
        s = z + k * inward

        def body(n, carry):
            kb, h = n // 2, lax.rem(n, 2)
            acc[h, item] += jnp.dot(
                aall[s * per + kb, h], ball[s, item, kb], preferred_element_type=jnp.float32
            )
            return carry

        lax.fori_loop(0, 2 * per, body, 0)

    def other_part(k, h):
        s = z + k * inward

        def body(kb, carry):
            pacc[h] += jnp.dot(
                oall[s * per + kb, h], ball[s, 0, kb], preferred_element_type=jnp.float32
            )
            return carry

        lax.fori_loop(0, per, body, 0)

    def p_copy(h):
        return remote(pacc.at[h], pin.at[h], p_send.at[h], p_recv.at[h], to_out)

    @pl.when(inner)
    def _():
        for h in range(2):
            o_in(h).wait_recv()
        o_first(lambda h: oall.at[p, h])
        arrived(1, 1)
        begin(middle, z_copy, 1, 1, True)
        arrived(2, 1)
        begin(middle, z_copy, 2, 1, True)

    a_third()

    @pl.when(inner)
    def _():
        arrived(1, -1)
        begin(middle, z_copy, 1, -1)

    a_last()
    own_a.wait()
    own_b.wait()
    ladder_part(0, 0)
    ladder_part(0, 1)

    @pl.when(inner)
    def _():
        arrived(2, -1)
        begin(middle, z_copy, 2, -1)
        arrived(1, 2)
        begin(middle, z_copy, 1, 2, True)
        o_second()
        arrived(0, -1)
        begin(middle, z_copy, 0, -1)
        arrived(2, 2)
        begin(middle, z_copy, 2, 2, True)
        o_third()
        ladder_part(-1, 0)
        ladder_part(-1, 1)
        ladder_part(1, 1)
        ladder_part(2, 1)
        arrived(0, 1)
        ladder_part(1, 0)
        o_last()
        for k in (0, 1):
            for h in range(2):
                other_part(k, h)

    @pl.when(outer)
    def _():
        for k in range(1, nz):
            arrived(1, k)
            ladder_part(k, 1)
            arrived(2, k)

    cols = cyc_ref.shape[1]
    width = 1024
    bounds = [(c, min(c + width, cols)) for c in range(0, cols, width)]
    rows = rall.shape[0] * rall.shape[1] * rall.shape[2]
    for lo, hi in bounds:
        r = rall[:, :, :, lo:hi].reshape(rows, hi - lo)
        total = jnp.dot(ci_ref[...], r, preferred_element_type=jnp.float32)
        keep = rl_ref[...] == cl_ref[:, lo:hi]
        cyc_ref[:, lo:hi] = jnp.where(keep, total, 0.0).astype(cyc_ref.dtype)

    @pl.when(inner)
    def _():
        arrived(0, 2)
        for h in range(2):
            other_part(2, h)
            begin(middle, p_copy, h)
        ladder_part(2, 0)

    hr = lad_ref.shape[0] // 2
    hc = lad_ref.shape[1] // 2
    for h in range(2):
        lad_ref[h * hr:(h + 1) * hr, hc:] = acc[h, 1].astype(lad_ref.dtype)

    @pl.when(inner)
    def _():
        for h in range(2):
            lad_ref[h * hr:(h + 1) * hr, :hc] = acc[h, 0].astype(lad_ref.dtype)

    @pl.when(outer)
    def _():
        for h in range(2):
            p_copy(h).wait_recv()
            lad_ref[h * hr:(h + 1) * hr, :hc] = (acc[h, 0] + pin[h]).astype(lad_ref.dtype)

    for c in common:
        c().wait_send()

    @pl.when(inner)
    def _():
        for c in middle:
            c().wait_send()

    @pl.when(outer)
    def _():
        for c in ends:
            c().wait_send()


def shards(nz, npl, amplitudes, integrals, cycle_integrals, occ_irrep, vir_irrep):
    rows, kb = amplitudes.shape
    occ = rows // NO
    n = integrals.shape[1]
    per = npl // nz
    occ_here = JW // npl
    columns = occ_here * NV
    crow = cycle_integrals.shape[0]
    a = amplitudes.reshape(2, rows // 2, kb)
    b = integrals.reshape(per, kb, 2, n // 2).transpose(2, 0, 1, 3)
    s = (
        amplitudes.reshape(occ, NO, kb)[:, :JW]
        .reshape(occ, npl, occ_here, kb)
        .transpose(1, 0, 2, 3)
        .reshape(npl, occ, columns)
    )
    ci = cycle_integrals.reshape(crow, nz, occ, CW).transpose(0, 1, 3, 2).reshape(crow, -1)
    row_label, col_label = masks(crow, columns, occ_irrep, vir_irrep)
    bf = jnp.bfloat16
    dma = pltpu.SemaphoreType.DMA
    return pl.pallas_call(
        kernel,
        out_shape=(
            jax.ShapeDtypeStruct((rows, n), bf),
            jax.ShapeDtypeStruct((crow, columns), bf),
        ),
        in_specs=[pl.BlockSpec(memory_space=pltpu.VMEM)] * 6,
        out_specs=(pl.BlockSpec(memory_space=pltpu.VMEM),) * 2,
        scratch_shapes=[
            pltpu.VMEM((npl, 2, rows // 2, kb), bf),
            pltpu.VMEM((npl, 2, rows // 2, kb), bf),
            pltpu.VMEM((nz, 2, per, kb, n // 2), bf),
            pltpu.VMEM((nz, npl, occ, columns), bf),
            pltpu.VMEM((2, 2, rows // 2, n // 2), jnp.float32),
            pltpu.VMEM((2, rows // 2, n // 2), jnp.float32),
            pltpu.VMEM((2, rows // 2, n // 2), jnp.float32),
            dma((3,)),
            dma((npl,)),
            dma((npl,)),
            dma((3, npl, 2)),
            dma((npl, 2)),
            dma((3, npl, 2)),
            dma((npl, 2)),
            dma((3, nz, 2)),
            dma((3, nz)),
            dma((2,)),
            dma((2,)),
            dma((2,)),
        ],
        compiler_params=pltpu.CompilerParams(
            collective_id=0, has_side_effects=True, vmem_limit_bytes=62 * 1024 * 1024
        ),
    )(a, b, s, ci, row_label, col_label)


def solution(mesh):
    nz, nx, nd = mesh.shape["row"], mesh.shape["col"], mesh.shape["depth"]
    npl = nx * nd
    if nx == 2 and nd == 4 and npl == CW and nz == 4:
        body = functools.partial(shards, nz, npl)
    else:
        body = general
    in_specs = (P("row", ("col", "depth")), P("row", ("col", "depth")), P("row", None), P(), P())
    out_specs = (P("row", ("col", "depth")), P("row", ("col", "depth")))
    return jax.shard_map(body, mesh=mesh, in_specs=in_specs, out_specs=out_specs, check_vma=False)
```

time: 209 us -> 176 us (0.84)
  Pallas kernels: 191 us -> 158 us
    pallas_call x1, Pallas kernels: 191 us -> 158 us  [shards(): pl.pallas_call(kernel, out_shape=(jax.ShapeDtypeStruct((rows, n), bf), ja...]
where the time goes in v2:
time: 176 us
  Pallas kernels  158 us (90%)
  local copies, waits for them, and re-layouts  17 us (10%)
    pallas_call x1, Pallas kernels, shards(): pl.pallas_call(kernel, out_shape=(jax.ShapeDtypeStruct((rows, n), bf), ja...  158 us
    unnamed x14, local copies, waits for them, and re-layouts  5.99 us
    reshape x2, local copies, waits for them, and re-layouts, shards(): b = integrals.reshape(per, kb, 2, n // 2).transpose(2, 0, 1, 3)  5.93 us

profile of v2, /device:TPU:0, one launch (start us, length us, event | category | flops | bytes accessed | tf_op | source)
XLA Modules:
  0.0 176.2 jit_solution(10378962742479472326)
XLA Ops:
  0.6 2.8 %copy.10 = bf16[800,900]{1,0:T(8,128)(2,1)S(1)} copy(bf16[800,900]{0,1:T(8,128)(2,1)} %param.5) | data formatting | bytes 2880000 | tf_op args[0]
  3.4 0.0 copy-start
  3.4 4.4 %reshape.76 = bf16[2,900,2,256]{3,2,1,0:T(2,128)(2,1)S(1)} reshape(bf16[1800,512]{1,0:T(8,128)(2,1)} %param.6) | data formatting | bytes 3686400 | tf_op jit(solution)/shard_map/reshape | solution.py:336
  7.8 1.5 copy.20
  9.3 0.0 copy-done
  9.3 0.4 reshape.77
  9.8 0.1 slice_bitcast_fusion
  9.9 0.0 copy-start.2
  9.9 0.0 copy-start.4
  9.9 0.0 slice-start
  9.9 0.0 copy-start.3
  9.9 1.3 reshape.82
  11.2 1.0 copy.18.s_ref
  12.2 0.0 copy-done.2
  12.2 0.1 copy.14
  12.4 0.7 copy.16.ci_ref
  13.1 0.0 copy-done.4
  13.1 0.1 fusion
  13.2 0.0 slice-done
  13.2 0.1 broadcast_xor_fusion.1
  13.2 0.7 xor.54.rl_ref
  13.9 0.0 copy-done.3
  13.9 0.1 broadcast_xor_fusion
  14.0 0.7 xor.53.cl_ref
  14.7 158.3 %shard_map.68 = (bf16[800,512]{1,0:T(8,128)(2,1)}, bf16[64,7200]{1,0:T(8,128)(2,1)}) custom-call(bf16[2,400,900]{2,1,0:T(8,128)(2,1)} %bitcast.16, bf16[2,2,900,256]{3,2,1,0:T(8,128)(2,1)} %bitcast.17, bf16[8,8,7200]{2,1,0:T(8,128)(2,1)} %copy.18.s_ref, bf16[64,256]{1,0:T(8,128)(2,1)} %copy.16.ci_ref, s32[64,1]{1,0:T(8,128)} %xor.54.rl_ref, ...), custom_call_target="tpu_custom_call" | custom-call | tf_op jit(solution)/shard_map/pallas_call | solution.py:347
  173.0 0.0 copy-start.1
  173.1 2.2 %copy.23 = bf16[800,512]{1,0:T(8,128)(2,1)} copy(bf16[800,512]{1,0:T(8,128)(2,1)} %get-tuple-element.6) | data formatting | bytes 1638400
  175.2 0.0 copy-done.1
  175.2 0.9 copy.24
  (1 shorter events, 0.0 us)
Async XLA Ops:
  3.4 6.0 %copy-start = (bf16[800,900]{1,0:T(8,128)(2,1)}, bf16[800,900]{1,0:T(8,128)(2,1)S(1)}, u32[]{:S(2)}) copy-start(bf16[800,900]{1,0:T(8,128)(2,1)S(1)} %copy.10) | copy-start | bytes 4320004
  9.9 2.4 %copy-start.2 = (bf16[64,256]{1,0:T(8,128)(2,1)S(1)}, bf16[64,256]{1,0:T(8,128)(2,1)}, u32[]{:S(2)}) copy-start(bf16[64,256]{1,0:T(8,128)(2,1)} %param.7) | copy-start | bytes 98308
  9.9 3.2 %copy-start.4 = (s32[100]{0:T(128)S(1)}, s32[100]{0:T(128)}, u32[]{:S(2)}) copy-start(s32[100]{0:T(128)} %param.8) | copy-start | bytes 1204
  9.9 3.3 %slice-start = ((s32[900]{0:T(1024)}), s32[8]{0:T(128)S(1)}, s32[]{:S(2)}) async-start(s32[900]{0:T(1024)} %param.9), calls=%async_computation | async-start | bytes 1024 | tf_op jit(solution)/shard_map/slice | solution.py:22
  9.9 4.0 %copy-start.3 = (s32[900]{0:T(1024)S(1)}, s32[900]{0:T(1024)}, u32[]{:S(2)}) copy-start(s32[900]{0:T(1024)} %param.9) | copy-start | bytes 10804
  173.0 2.2 %copy-start.1 = (bf16[64,7200]{1,0:T(8,128)(2,1)S(1)}, bf16[64,7200]{1,0:T(8,128)(2,1)}, u32[]{:S(2)}) copy-start(bf16[64,7200]{1,0:T(8,128)(2,1)} %get-tuple-element.7) | copy-start | bytes 2764804

commit v3 on v2

--- a/solution.py
+++ b/solution.py
@@ -90,13 +90,22 @@
         pl.semaphore_signal(barrier, inc=1, device_id=to_out, device_id_type=MESH)
 
     own_a = pltpu.make_async_copy(a_ref, aall.at[p], loc_sem.at[0])
-    own_b = pltpu.make_async_copy(b_ref, ball.at[z], loc_sem.at[1])
-    own_s = pltpu.make_async_copy(s_ref.at[p], rall.at[z, p], loc_sem.at[2])
+    wide = ball.shape[3]
+    nc = ball.shape[1]
+    direct = nc - 1
+
+    def b_part(c):
+        return b_ref.at[:, c * wide:(c + 1) * wide]
+
+    own_b = [pltpu.make_async_copy(b_part(c), ball.at[z, c], loc_sem.at[2 + c]) for c in range(nc)]
+    own_s = pltpu.make_async_copy(s_ref.at[p], rall.at[z, p], loc_sem.at[1])
     own_a.start()
-    own_b.start()
+    for c in own_b:
+        c.start()
     own_s.start()
     pl.semaphore_wait(barrier, npl + inner.astype(jnp.int32))
 
+    half = npl // 2
     common, middle, ends = [], [], []
 
     def begin(kept, make, *args, **kw):
@@ -105,7 +114,10 @@
 
     def z_copy(item, k, outwards=False, src=None):
         s = z + k * inward
-        dst = rall.at[s] if item == 2 else ball.at[s, item]
+        if item < nc:
+            dst = ball.at[s, item]
+        else:
+            dst = rall.at[s, pl.ds((item - nc) * half, half)]
         d = 1 if outwards else 0
         return remote(dst if src is None else src(), dst, z_send.at[item, s, d],
                       z_recv.at[item, s], to_out if outwards else to_in)
@@ -123,16 +135,16 @@
     for i in range(1, npl):
         begin(common, s_out, i)
 
+    begin(common, z_copy, direct, 0, src=lambda: b_part(direct))
+
+    @pl.when(inner)
+    def _():
+        begin(middle, z_copy, direct, 0, True, src=lambda: b_part(direct))
+
     @pl.when(outer)
     def _():
         for h in range(2):
             begin(ends, o_in, h)
-
-    begin(common, z_copy, 1, 0, src=lambda: b_ref.at[1])
-
-    @pl.when(inner)
-    def _():
-        begin(middle, z_copy, 1, 0, True, src=lambda: b_ref.at[1])
 
     q_x = (1 - x) * nd + dep
     q_y = x * nd + (1 - y) * 2 + core
@@ -164,9 +176,9 @@
 
         def third():
             copy(q_d, 0, "y").wait_recv()
-            begin(kept, copy, q_d, 0, "p")
+            copy(q_d, 0, "p").start()
             copy(q_d, 1, "x").wait_recv()
-            begin(kept, copy, q_d, 1, "p")
+            copy(q_d, 1, "p").start()
 
         def last():
             for q in (p, q_x, q_y, q_d):
@@ -174,6 +186,8 @@
                 for h in range(2):
                     copy(other, h, "p").wait_recv()
 
+        for h in range(2):
+            kept.append(functools.partial(copy, q_d, h, "p"))
         return first, second, third, last
 
     a_first, a_second, a_third, a_last = plane(aall, a_send, a_recv, common)
@@ -185,130 +199,144 @@
     for i in range(1, npl):
         q, dev = peer(i)
         remote(s_ref.at[p], rall.at[z, q], s_send.at[i], s_recv.at[q], dev).wait_recv()
-    begin(common, z_copy, 2, 0)
-
-    @pl.when(inner)
-    def _():
-        begin(middle, z_copy, 2, 0, True)
-
-    begin(common, z_copy, 0, 0, src=lambda: b_ref.at[0])
-
-    a_second()
+    regrouped = (nc, nc + 1)
+    for item in regrouped:
+        begin(common, z_copy, item, 0)
+
+    def forward(item, k, outwards):
+        arrived(item, k)
+        begin(middle, z_copy, item, k, outwards)
+
+    @pl.when(inner)
+    def _():
+        for item in regrouped:
+            begin(middle, z_copy, item, 0, True)
+        forward(direct, -1, False)
+        forward(direct, 1, True)
+
+    def own_chunk(c):
+        return z_copy(c, 0, src=lambda: b_part(c))
+
+    for c in range(direct):
+        begin(common, own_chunk, c)
+
     acc[...] = jnp.zeros_like(acc)
     pacc[...] = jnp.zeros_like(pacc)
-
-    def ladder_part(k, item):
+    kb_rows = aall.shape[3]
+
+    def chunk(s, c, kb):
+        return ball[s, c, kb * kb_rows:(kb + 1) * kb_rows, :]
+
+    def ladder_pair(k, c):
         s = z + k * inward
-
-        def body(n, carry):
-            kb, h = n // 2, lax.rem(n, 2)
-            acc[h, item] += jnp.dot(
-                aall[s * per + kb, h], ball[s, item, kb], preferred_element_type=jnp.float32
-            )
-            return carry
-
-        lax.fori_loop(0, 2 * per, body, 0)
-
-    def other_part(k, h):
+        for kb in range(per):
+            both = jnp.concatenate([chunk(s, c, kb), chunk(s, c + 1, kb)], axis=1)
+
+            def body(h, carry):
+                r = jnp.dot(aall[s * per + kb, h], both, preferred_element_type=jnp.float32)
+                acc[h, c] += r[:, :wide]
+                acc[h, c + 1] += r[:, wide:]
+                return carry
+
+            lax.fori_loop(0, 2, body, 0)
+
+    def single(total, buf, k, c):
         s = z + k * inward
-
-        def body(kb, carry):
-            pacc[h] += jnp.dot(
-                oall[s * per + kb, h], ball[s, 0, kb], preferred_element_type=jnp.float32
-            )
-            return carry
-
-        lax.fori_loop(0, per, body, 0)
-
-    def p_copy(h):
-        return remote(pacc.at[h], pin.at[h], p_send.at[h], p_recv.at[h], to_out)
-
-    @pl.when(inner)
-    def _():
+        for kb in range(per):
+            one = chunk(s, c, kb)
+
+            def body(h, carry):
+                total[h, c] += jnp.dot(buf[s * per + kb, h], one, preferred_element_type=jnp.float32)
+                return carry
+
+            lax.fori_loop(0, 2, body, 0)
+
+    def p_copy(c):
+        return remote(pacc.at[:, c], pin.at[:, c], p_send.at[c], p_recv.at[c], to_out)
+
+    def cycle_all():
+        cols = cyc_ref.shape[1]
+        width = 1024
+        rows = rall.shape[0] * rall.shape[1] * rall.shape[2]
+        for lo in range(0, cols, width):
+            hi = min(lo + width, cols)
+            r = rall[:, :, :, lo:hi].reshape(rows, hi - lo)
+            total = jnp.dot(ci_ref[...], r, preferred_element_type=jnp.float32)
+            keep = rl_ref[...] == cl_ref[:, lo:hi]
+            cyc_ref[:, lo:hi] = jnp.where(keep, total, 0.0).astype(cyc_ref.dtype)
+
+    own_a.wait()
+    for c in own_b:
+        c.wait()
+    hr = lad_ref.shape[0] // 2
+
+    def put(h, c, value):
+        lad_ref[h * hr:(h + 1) * hr, c * wide:(c + 1) * wide] = value.astype(lad_ref.dtype)
+
+    @pl.when(inner)
+    def _():
+        for item in regrouped:
+            forward(item, 1, True)
         for h in range(2):
             o_in(h).wait_recv()
         o_first(lambda h: oall.at[p, h])
-        arrived(1, 1)
-        begin(middle, z_copy, 1, 1, True)
-        arrived(2, 1)
-        begin(middle, z_copy, 2, 1, True)
-
-    a_third()
-
-    @pl.when(inner)
-    def _():
-        arrived(1, -1)
-        begin(middle, z_copy, 1, -1)
-
-    a_last()
-    own_a.wait()
-    own_b.wait()
-    ladder_part(0, 0)
-    ladder_part(0, 1)
-
-    @pl.when(inner)
-    def _():
-        arrived(2, -1)
-        begin(middle, z_copy, 2, -1)
-        arrived(1, 2)
-        begin(middle, z_copy, 1, 2, True)
+        forward(direct, 2, True)
+        for item in regrouped:
+            forward(item, -1, False)
         o_second()
-        arrived(0, -1)
-        begin(middle, z_copy, 0, -1)
-        arrived(2, 2)
-        begin(middle, z_copy, 2, 2, True)
+
+    a_second()
+
+    @pl.when(inner)
+    def _():
+        for c in range(direct):
+            forward(c, -1, False)
+        for item in regrouped:
+            forward(item, 2, True)
+
+    @pl.when(outer)
+    def _():
+        a_third()
+        a_last()
+        for c in range(0, nc, 2):
+            ladder_pair(0, c)
+        for k in range(1, nz):
+            arrived(direct, k)
+            single(acc, aall, k, direct)
+            for item in regrouped:
+                arrived(item, k)
+
+    cycle_all()
+
+    @pl.when(inner)
+    def _():
         o_third()
-        ladder_part(-1, 0)
-        ladder_part(-1, 1)
-        ladder_part(1, 1)
-        ladder_part(2, 1)
-        arrived(0, 1)
-        ladder_part(1, 0)
         o_last()
-        for k in (0, 1):
+        for c in range(direct):
+            single(pacc, oall, 0, c)
+            arrived(c, 1)
+            single(pacc, oall, 1, c)
+            arrived(c, 2)
+            single(pacc, oall, 2, c)
+            begin(middle, p_copy, c)
+            if c == direct - 2:
+                a_third()
+        a_last()
+        for k in (0, -1, 1, 2):
+            for c in range(0, nc, 2):
+                ladder_pair(k, c)
+        for h in range(2):
+            for c in range(nc):
+                put(h, c, acc[h, c])
+
+    @pl.when(outer)
+    def _():
+        for h in range(2):
+            put(h, direct, acc[h, direct])
+        for c in range(direct):
+            p_copy(c).wait_recv()
             for h in range(2):
-                other_part(k, h)
-
-    @pl.when(outer)
-    def _():
-        for k in range(1, nz):
-            arrived(1, k)
-            ladder_part(k, 1)
-            arrived(2, k)
-
-    cols = cyc_ref.shape[1]
-    width = 1024
-    bounds = [(c, min(c + width, cols)) for c in range(0, cols, width)]
-    rows = rall.shape[0] * rall.shape[1] * rall.shape[2]
-    for lo, hi in bounds:
-        r = rall[:, :, :, lo:hi].reshape(rows, hi - lo)
-        total = jnp.dot(ci_ref[...], r, preferred_element_type=jnp.float32)
-        keep = rl_ref[...] == cl_ref[:, lo:hi]
-        cyc_ref[:, lo:hi] = jnp.where(keep, total, 0.0).astype(cyc_ref.dtype)
-
-    @pl.when(inner)
-    def _():
-        arrived(0, 2)
-        for h in range(2):
-            other_part(2, h)
-            begin(middle, p_copy, h)
-        ladder_part(2, 0)
-
-    hr = lad_ref.shape[0] // 2
-    hc = lad_ref.shape[1] // 2
-    for h in range(2):
-        lad_ref[h * hr:(h + 1) * hr, hc:] = acc[h, 1].astype(lad_ref.dtype)
-
-    @pl.when(inner)
-    def _():
-        for h in range(2):
-            lad_ref[h * hr:(h + 1) * hr, :hc] = acc[h, 0].astype(lad_ref.dtype)
-
-    @pl.when(outer)
-    def _():
-        for h in range(2):
-            p_copy(h).wait_recv()
-            lad_ref[h * hr:(h + 1) * hr, :hc] = (acc[h, 0] + pin[h]).astype(lad_ref.dtype)
+                put(h, c, acc[h, c] + pin[h, c])
 
     for c in common:
         c().wait_send()
@@ -328,12 +356,12 @@
     rows, kb = amplitudes.shape
     occ = rows // NO
     n = integrals.shape[1]
-    per = npl // nz
     occ_here = JW // npl
     columns = occ_here * NV
     crow = cycle_integrals.shape[0]
     a = amplitudes.reshape(2, rows // 2, kb)
-    b = integrals.reshape(per, kb, 2, n // 2).transpose(2, 0, 1, 3)
+    nc = n // 128
+    b = integrals
     s = (
         amplitudes.reshape(occ, NO, kb)[:, :JW]
         .reshape(occ, npl, occ_here, kb)
@@ -350,28 +378,29 @@
             jax.ShapeDtypeStruct((rows, n), bf),
             jax.ShapeDtypeStruct((crow, columns), bf),
         ),
-        in_specs=[pl.BlockSpec(memory_space=pltpu.VMEM)] * 6,
+        in_specs=[pl.BlockSpec(memory_space=pltpu.VMEM), pl.BlockSpec(memory_space=pl.ANY)]
+        + [pl.BlockSpec(memory_space=pltpu.VMEM)] * 4,
         out_specs=(pl.BlockSpec(memory_space=pltpu.VMEM),) * 2,
         scratch_shapes=[
             pltpu.VMEM((npl, 2, rows // 2, kb), bf),
             pltpu.VMEM((npl, 2, rows // 2, kb), bf),
-            pltpu.VMEM((nz, 2, per, kb, n // 2), bf),
+            pltpu.VMEM((nz, nc, integrals.shape[0], n // nc), bf),
             pltpu.VMEM((nz, npl, occ, columns), bf),
-            pltpu.VMEM((2, 2, rows // 2, n // 2), jnp.float32),
-            pltpu.VMEM((2, rows // 2, n // 2), jnp.float32),
-            pltpu.VMEM((2, rows // 2, n // 2), jnp.float32),
-            dma((3,)),
+            pltpu.VMEM((2, nc, rows // 2, n // nc), jnp.float32),
+            pltpu.VMEM((2, nc - 1, rows // 2, n // nc), jnp.float32),
+            pltpu.VMEM((2, nc - 1, rows // 2, n // nc), jnp.float32),
+            dma((2 + nc,)),
             dma((npl,)),
             dma((npl,)),
             dma((3, npl, 2)),
             dma((npl, 2)),
             dma((3, npl, 2)),
             dma((npl, 2)),
-            dma((3, nz, 2)),
-            dma((3, nz)),
+            dma((nc + 2, nz, 2)),
+            dma((nc + 2, nz)),
             dma((2,)),
-            dma((2,)),
-            dma((2,)),
+            dma((nc - 1,)),
+            dma((nc - 1,)),
         ],
         compiler_params=pltpu.CompilerParams(
             collective_id=0, has_side_effects=True, vmem_limit_bytes=62 * 1024 * 1024

time: 176 us -> 168 us (0.955)
  Pallas kernels: 158 us -> 154 us
  local copies, waits for them, and re-layouts: 17 us -> 13.2 us
    reshape x2 -> x0, local copies, waits for them, and re-layouts: 5.93 us -> none  [shards(): b = integrals.reshape(per, kb, 2, n // 2).transpose(2, 0, 1, 3)]
    pallas_call x1, Pallas kernels: 158 us -> 154 us  [shards(): pl.pallas_call(kernel, out_shape=(jax.ShapeDtypeStruct((rows, n), bf), ja...]
where the time goes in v3:
time: 168 us
  Pallas kernels  154 us (92%)
  local copies, waits for them, and re-layouts  13.2 us (8%)
    pallas_call x1, Pallas kernels, shards(): pl.pallas_call(kernel, out_shape=(jax.ShapeDtypeStruct((rows, n), bf), ja...  154 us
    unnamed x14, local copies, waits for them, and re-layouts  5.98 us
    reshape x2, local copies, waits for them, and re-layouts, shards(): s = amplitudes.reshape(occ, NO, kb)[:, :JW].reshape(occ, npl, occ_here, k...  3.5 us

profile of v3, /device:TPU:0, one launch (start us, length us, event | category | flops | bytes accessed | tf_op | source)
XLA Modules:
  0.0 167.8 jit_solution(6280028398274165097)
XLA Ops:
  0.6 2.8 %copy.10 = bf16[800,900]{1,0:T(8,128)(2,1)S(1)} copy(bf16[800,900]{0,1:T(8,128)(2,1)} %param.5) | data formatting | bytes 2880000 | tf_op args[0]
  3.4 0.0 copy-start
  3.4 0.5 reshape.73
  3.9 1.1 slice_bitcast_fusion
  4.9 0.0 copy-done
  4.9 0.0 copy-start.2
  4.9 0.0 copy-start.4
  4.9 0.0 slice-start
  5.0 0.0 copy-start.3
  5.0 2.5 %reshape.78 = bf16[8,8,7200]{2,0,1:T(8,128)(2,1)S(1)} reshape(bf16[8,8,8,900]{3,2,0,1:T(8,128)(2,1)} %slice_bitcast_fusion) | data formatting | bytes 1843200 | tf_op jit(solution)/shard_map/reshape | solution.py:369
  7.4 1.0 copy.17.s_ref
  8.5 0.0 copy-done.2
  8.5 0.1 copy.13
  8.6 0.7 copy.15.ci_ref
  9.3 0.0 copy-done.4
  9.3 0.1 fusion
  9.4 0.0 slice-done
  9.4 0.1 broadcast_xor_fusion.1
  9.5 0.7 xor.54.rl_ref
  10.2 0.0 copy-done.3
  10.2 0.1 broadcast_xor_fusion
  10.2 0.7 xor.53.cl_ref
  10.9 153.8 %shard_map.68 = (bf16[800,512]{1,0:T(8,128)(2,1)}, bf16[64,7200]{1,0:T(8,128)(2,1)}) custom-call(bf16[2,400,900]{2,1,0:T(8,128)(2,1)} %bitcast.13, bf16[1800,512]{1,0:T(8,128)(2,1)} %b_ref.1, bf16[8,8,7200]{2,1,0:T(8,128)(2,1)} %copy.17.s_ref, bf16[64,256]{1,0:T(8,128)(2,1)} %copy.15.ci_ref, s32[64,1]{1,0:T(8,128)} %xor.54.rl_ref, s32[1,7200]{1,0:T(1,128)} %xor.53.cl_ref), custom_call_target="tpu_custom_call" | custom-call | tf_op jit(solution)/shard_map/pallas_call | solution.py:375
  164.7 0.0 copy-start.1
  164.7 2.2 %copy.20 = bf16[800,512]{1,0:T(8,128)(2,1)} copy(bf16[800,512]{1,0:T(8,128)(2,1)} %get-tuple-element.6) | data formatting | bytes 1638400
  166.9 0.0 copy-done.1
  166.9 0.9 copy.21
  (1 shorter events, 0.0 us)
Async XLA Ops:
  3.4 1.6 copy-start
  4.9 3.5 %copy-start.2 = (bf16[64,256]{1,0:T(8,128)(2,1)S(1)}, bf16[64,256]{1,0:T(8,128)(2,1)}, u32[]{:S(2)}) copy-start(bf16[64,256]{1,0:T(8,128)(2,1)} %param.7) | copy-start | bytes 98308
  4.9 4.4 %copy-start.4 = (s32[100]{0:T(128)S(1)}, s32[100]{0:T(128)}, u32[]{:S(2)}) copy-start(s32[100]{0:T(128)} %param.8) | copy-start | bytes 1204
  4.9 4.5 %slice-start = ((s32[900]{0:T(1024)}), s32[8]{0:T(128)S(1)}, s32[]{:S(2)}) async-start(s32[900]{0:T(1024)} %param.9), calls=%async_computation | async-start | bytes 1024 | tf_op jit(solution)/shard_map/slice | solution.py:22
  5.0 5.2 %copy-start.3 = (s32[900]{0:T(1024)S(1)}, s32[900]{0:T(1024)}, u32[]{:S(2)}) copy-start(s32[900]{0:T(1024)} %param.9) | copy-start | bytes 10804
  164.7 2.2 %copy-start.1 = (bf16[64,7200]{1,0:T(8,128)(2,1)S(1)}, bf16[64,7200]{1,0:T(8,128)(2,1)}, u32[]{:S(2)}) copy-start(bf16[64,7200]{1,0:T(8,128)(2,1)} %get-tuple-element.7) | copy-start | bytes 2764804

commit v4 on v3

--- a/solution.py
+++ b/solution.py
@@ -162,17 +162,15 @@
                 for way in ("x", "y", "p"):
                     begin(kept, copy, p, h, way, functools.partial(src, h))
 
+        def relay():
+            for h in range(2):
+                for q, way in ((q_x, "x"), (q_y, "y")):
+                    copy(q, h, way).wait_recv()
+                    copy(q, h, "p").start()
+
         def second():
-            copy(q_x, 0, "x").wait_recv()
-            begin(kept, copy, q_x, 0, "y")
-            begin(kept, copy, q_x, 0, "p")
-            copy(q_y, 0, "y").wait_recv()
-            begin(kept, copy, q_y, 0, "p")
-            copy(q_y, 1, "y").wait_recv()
-            begin(kept, copy, q_y, 1, "x")
-            begin(kept, copy, q_y, 1, "p")
-            copy(q_x, 1, "x").wait_recv()
-            begin(kept, copy, q_x, 1, "p")
+            copy(q_x, 0, "y").start()
+            copy(q_y, 1, "x").start()
 
         def third():
             copy(q_d, 0, "y").wait_recv()
@@ -180,18 +178,23 @@
             copy(q_d, 1, "x").wait_recv()
             copy(q_d, 1, "p").start()
 
-        def last():
-            for q in (p, q_x, q_y, q_d):
+        def last(group):
+            for q in group:
                 other = q + 1 - 2 * core
                 for h in range(2):
                     copy(other, h, "p").wait_recv()
 
         for h in range(2):
-            kept.append(functools.partial(copy, q_d, h, "p"))
-        return first, second, third, last
-
-    a_first, a_second, a_third, a_last = plane(aall, a_send, a_recv, common)
-    o_first, o_second, o_third, o_last = plane(oall, o_send, o_recv, middle)
+            for q in (q_x, q_y, q_d):
+                kept.append(functools.partial(copy, q, h, "p"))
+        kept.append(functools.partial(copy, q_x, 0, "y"))
+        kept.append(functools.partial(copy, q_y, 1, "x"))
+        return first, relay, second, third, last
+
+    near = (p, q_x, q_y)
+
+    a_first, a_relay, a_second, a_third, a_last = plane(aall, a_send, a_recv, common)
+    o_first, o_relay, o_second, o_third, o_last = plane(oall, o_send, o_recv, middle)
 
     a_first(lambda h: a_ref.at[h])
 
@@ -273,6 +276,16 @@
     def put(h, c, value):
         lad_ref[h * hr:(h + 1) * hr, c * wide:(c + 1) * wide] = value.astype(lad_ref.dtype)
 
+    far = (1 - x) * 2 + (1 - y)
+
+    def slab(k, early):
+        s = z + k * inward
+
+        @pl.when((s != far) if early else (s == far))
+        def _():
+            for c in range(0, nc, 2):
+                ladder_pair(k, c)
+
     @pl.when(inner)
     def _():
         for item in regrouped:
@@ -280,9 +293,20 @@
         for h in range(2):
             o_in(h).wait_recv()
         o_first(lambda h: oall.at[p, h])
+
+    a_relay()
+
+    @pl.when(inner)
+    def _():
         forward(direct, 2, True)
         for item in regrouped:
             forward(item, -1, False)
+        a_last(near)
+        for c in range(direct):
+            arrived(c, 1)
+        slab(0, True)
+        slab(1, True)
+        o_relay()
         o_second()
 
     a_second()
@@ -297,7 +321,7 @@
     @pl.when(outer)
     def _():
         a_third()
-        a_last()
+        a_last(near + (q_d,))
         for c in range(0, nc, 2):
             ladder_pair(0, c)
         for k in range(1, nz):
@@ -311,20 +335,20 @@
     @pl.when(inner)
     def _():
         o_third()
-        o_last()
+        slab(-1, True)
+        o_last(near + (q_d,))
         for c in range(direct):
-            single(pacc, oall, 0, c)
-            arrived(c, 1)
-            single(pacc, oall, 1, c)
+            for k in range(2):
+                single(pacc, oall, k, c)
             arrived(c, 2)
             single(pacc, oall, 2, c)
             begin(middle, p_copy, c)
             if c == direct - 2:
                 a_third()
-        a_last()
+        slab(2, True)
+        a_last((q_d,))
         for k in (0, -1, 1, 2):
-            for c in range(0, nc, 2):
-                ladder_pair(k, c)
+            slab(k, False)
         for h in range(2):
             for c in range(nc):
                 put(h, c, acc[h, c])
@@ -378,8 +402,8 @@
             jax.ShapeDtypeStruct((rows, n), bf),
             jax.ShapeDtypeStruct((crow, columns), bf),
         ),
-        in_specs=[pl.BlockSpec(memory_space=pltpu.VMEM), pl.BlockSpec(memory_space=pl.ANY)]
-        + [pl.BlockSpec(memory_space=pltpu.VMEM)] * 4,
+        in_specs=[pl.BlockSpec(memory_space=pl.ANY)] * 3
+        + [pl.BlockSpec(memory_space=pltpu.VMEM)] * 3,
         out_specs=(pl.BlockSpec(memory_space=pltpu.VMEM),) * 2,
         scratch_shapes=[
             pltpu.VMEM((npl, 2, rows // 2, kb), bf),

time: 168 us -> 167 us (level)
  no operation moved by 1% of the time
where the time goes in v4:
time: 167 us
  Pallas kernels  153 us (92%)
  local copies, waits for them, and re-layouts  13.2 us (8%)
    pallas_call x1, Pallas kernels, shards(): pl.pallas_call(kernel, out_shape=(jax.ShapeDtypeStruct((rows, n), bf), ja...  153 us
    unnamed x14, local copies, waits for them, and re-layouts  5.98 us
    reshape x2, local copies, waits for them, and re-layouts, shards(): s = amplitudes.reshape(occ, NO, kb)[:, :JW].reshape(occ, npl, occ_here, k...  3.5 us

profile of v4, /device:TPU:0, one launch (start us, length us, event | category | flops | bytes accessed | tf_op | source)
XLA Modules:
  0.0 166.9 jit_solution(3620704549799009795)
XLA Ops:
  0.6 2.8 %copy.10 = bf16[800,900]{1,0:T(8,128)(2,1)S(1)} copy(bf16[800,900]{0,1:T(8,128)(2,1)} %param.5) | data formatting | bytes 2880000 | tf_op args[0]
  3.4 0.0 copy-start
  3.4 0.5 reshape.73
  3.9 1.1 slice_bitcast_fusion
  4.9 0.0 copy-done
  4.9 0.0 copy-start.2
  4.9 0.0 copy-start.4
  4.9 0.0 slice-start
  5.0 0.0 copy-start.3
  5.0 2.5 %reshape.78 = bf16[8,8,7200]{2,0,1:T(8,128)(2,1)S(1)} reshape(bf16[8,8,8,900]{3,2,0,1:T(8,128)(2,1)} %slice_bitcast_fusion) | data formatting | bytes 1843200 | tf_op jit(solution)/shard_map/reshape | solution.py:393
  7.4 1.0 copy.17.s_ref
  8.5 0.0 copy-done.2
  8.5 0.1 copy.13
  8.6 0.7 copy.15.ci_ref
  9.3 0.0 copy-done.4
  9.3 0.1 fusion
  9.4 0.0 slice-done
  9.4 0.1 broadcast_xor_fusion.1
  9.5 0.7 xor.54.rl_ref
  10.2 0.0 copy-done.3
  10.2 0.1 broadcast_xor_fusion
  10.2 0.7 xor.53.cl_ref
  10.9 152.9 %shard_map.68 = (bf16[800,512]{1,0:T(8,128)(2,1)}, bf16[64,7200]{1,0:T(8,128)(2,1)}) custom-call(bf16[2,400,900]{2,1,0:T(8,128)(2,1)} %bitcast.13, bf16[1800,512]{1,0:T(8,128)(2,1)} %b_ref.1, bf16[8,8,7200]{2,1,0:T(8,128)(2,1)} %copy.17.s_ref, bf16[64,256]{1,0:T(8,128)(2,1)} %copy.15.ci_ref, s32[64,1]{1,0:T(8,128)} %xor.54.rl_ref, s32[1,7200]{1,0:T(1,128)} %xor.53.cl_ref), custom_call_target="tpu_custom_call" | custom-call | tf_op jit(solution)/shard_map/pallas_call | solution.py:399
  163.8 0.0 copy-start.1
  163.8 2.2 %copy.20 = bf16[800,512]{1,0:T(8,128)(2,1)} copy(bf16[800,512]{1,0:T(8,128)(2,1)} %get-tuple-element.6) | data formatting | bytes 1638400
  166.0 0.0 copy-done.1
  166.0 0.9 copy.21
  (1 shorter events, 0.0 us)
Async XLA Ops:
  3.4 1.6 copy-start
  4.9 3.5 %copy-start.2 = (bf16[64,256]{1,0:T(8,128)(2,1)S(1)}, bf16[64,256]{1,0:T(8,128)(2,1)}, u32[]{:S(2)}) copy-start(bf16[64,256]{1,0:T(8,128)(2,1)} %param.7) | copy-start | bytes 98308
  4.9 4.4 %copy-start.4 = (s32[100]{0:T(128)S(1)}, s32[100]{0:T(128)}, u32[]{:S(2)}) copy-start(s32[100]{0:T(128)} %param.8) | copy-start | bytes 1204
  4.9 4.5 %slice-start = ((s32[900]{0:T(1024)}), s32[8]{0:T(128)S(1)}, s32[]{:S(2)}) async-start(s32[900]{0:T(1024)} %param.9), calls=%async_computation | async-start | bytes 1024 | tf_op jit(solution)/shard_map/slice | solution.py:22
  5.0 5.2 %copy-start.3 = (s32[900]{0:T(1024)S(1)}, s32[900]{0:T(1024)}, u32[]{:S(2)}) copy-start(s32[900]{0:T(1024)} %param.9) | copy-start | bytes 10804
  163.8 2.2 %copy-start.1 = (bf16[64,7200]{1,0:T(8,128)(2,1)S(1)}, bf16[64,7200]{1,0:T(8,128)(2,1)}, u32[]{:S(2)}) copy-start(bf16[64,7200]{1,0:T(8,128)(2,1)} %get-tuple-element.7) | copy-start | bytes 2764804
